TPU v7x, 512 devices: a whole 4x8x8 slice. The times are simulated.
512 devices in a mesh: lang: 64 (over y, z), rep: 8 (over x, core).
Axes of the slice: x: 4, y: 8, z: 8, core: 2. Of those that a mesh axis runs over, the one named last changes fastest.
Arguments:
- tokens: bfloat16 [65536, 1024], P(('lang', 'rep')), may hold values from -24 to 24
- grad_out: bfloat16 [65536, 1024], P(('lang', 'rep')), may hold values from -24 to 24
- lang_ids: int32 [65536], P(('lang', 'rep')), may hold values from 0 to 7, as said below
- slot_ids: int32 [65536], P(('lang', 'rep')), may hold values from 0 to 23, as said below
- w_up: bfloat16 [1024, 32768], P(None, 'lang'), may hold values from -0.1875 to 0.1875
- w_down_t: bfloat16 [1024, 32768], P(None, 'lang'), may hold values from -0.09375 to 0.09375
Outputs:
- ffn_out: bfloat16 [65536, 1024], P(('lang', 'rep'))
- grad_tokens: bfloat16 [65536, 1024], P(('lang', 'rep'))
- grad_up: float32 [1024, 32768], P('rep', 'lang')
- grad_down: float32 [1024, 32768], P('rep', 'lang')
Inputs may be any that keep to these rules, and one draw needn't show every extreme that they name: `lang_ids`: each device holds 128 consecutive tokens. On every device one language, the same on all devices, has exactly 24 tokens; every other language has at most 18 tokens on a device, and on every device one of them has exactly 18. `slot_ids`: on each device the tokens of one language hold the distinct slots 0 to their count minus 1, in no particular order.
All inputs are finite; a program needn't handle non-finite values.
Results may differ from a plain program's by a relative error of at most 0.0058.
Values may be sent and summed in bfloat16 or wider, within the bound.
A program may use at most 128 MiB of HBM per device.

v0:
```python
import jax
import jax.numpy as jnp
from jax import lax
from jax.sharding import PartitionSpec as P

MODULES = 8
TOK_DEV = 128
CAPACITY = 18


INV_ROOT_TWO = 0.7071067811865476
INV_ROOT_TAU = 0.3989422804014327


def gelu_value(values):
    return 0.5 * values * (1.0 + lax.erf(values * INV_ROOT_TWO))


def gelu_slope(values):
    return (
        0.5 * (1.0 + lax.erf(values * INV_ROOT_TWO))
        + values * jnp.exp(-0.5 * values * values) * INV_ROOT_TAU
    )


def per_device(tokens, grad_out, lang_ids, slot_ids, w_up, w_down_t):
    groups = lax.axis_size("lang") // MODULES
    feature_width = tokens.shape[1]
    hid_units = w_up.shape[1]
    capacity = CAPACITY
    keep_mask = slot_ids < capacity
    target = jnp.where(keep_mask, lang_ids * capacity + slot_ids, MODULES * capacity)
    safe_slot = jnp.minimum(slot_ids, capacity - 1)
    token_scale = 1.0 / TOK_DEV

    def place(values):
        buffer = (
            jnp.zeros((MODULES * capacity, feature_width), values.dtype)
            .at[target]
            .set(values, mode="drop")
        )
        return buffer.reshape(MODULES, capacity, feature_width)

    def dispatch(values):
        return jnp.repeat(place(values), groups, axis=0)

    def collect(returned):
        picked = returned.reshape(MODULES, groups, capacity, feature_width)[lang_ids, :, safe_slot]
        total_sum = jnp.sum(picked, axis=1, dtype=jnp.float32)
        return jnp.where(keep_mask[:, None], total_sum, 0.0).astype(jnp.bfloat16)

    received = lax.all_to_all(dispatch(tokens), "lang", split_axis=0, concat_axis=0, tiled=True)
    src_count, slot_count, _ = received.shape
    pre_rows = jnp.dot(
        received.reshape(-1, feature_width), w_up, preferred_element_type=jnp.float32
    )
    hidden_rows = gelu_value(pre_rows).astype(jnp.bfloat16)
    partial_rows = (
        lax.dot_general(
            hidden_rows, w_down_t, (((1,), (1,)), ((), ())), preferred_element_type=jnp.float32
        )
        .astype(jnp.bfloat16)
        .reshape(src_count, slot_count, feature_width)
    )
    returned = lax.all_to_all(partial_rows, "lang", split_axis=0, concat_axis=0, tiled=True)
    pre_act = pre_rows.reshape(src_count, slot_count, hid_units)
    hidden = hidden_rows.reshape(src_count, slot_count, hid_units)
    recv_grads = lax.all_to_all(dispatch(grad_out), "lang", split_axis=0, concat_axis=0, tiled=True)
    flat_tokens = received.reshape(-1, feature_width)
    flat_grads = recv_grads.reshape(-1, feature_width)
    pre_flat = pre_act.reshape(-1, hid_units)
    hidden_flat = hidden.reshape(-1, hid_units)
    sliced = flat_grads
    grad_down = lax.psum_scatter(
        lax.dot_general(
            sliced, hidden_flat, (((0,), (0,)), ((), ())), preferred_element_type=jnp.float32
        )
        * token_scale,
        "rep",
        scatter_dimension=0,
        tiled=True,
    )
    d_hidden = jnp.dot(flat_grads, w_down_t, preferred_element_type=jnp.float32)
    d_pre = (d_hidden * gelu_slope(pre_flat)).astype(jnp.bfloat16)
    sliced = flat_tokens
    grad_up = lax.psum_scatter(
        lax.dot_general(sliced, d_pre, (((0,), (0,)), ((), ())), preferred_element_type=jnp.float32)
        * token_scale,
        "rep",
        scatter_dimension=0,
        tiled=True,
    )
    dx_part = lax.dot_general(
        d_pre, w_up, (((1,), (1,)), ((), ())), preferred_element_type=jnp.float32
    ).astype(jnp.bfloat16)
    dx_part = dx_part.reshape(received.shape)
    dx_back = lax.all_to_all(dx_part, "lang", split_axis=0, concat_axis=0, tiled=True)
    return (collect(returned), collect(dx_back), grad_up, grad_down)


def solution(mesh):
    placed = (
        P(("lang", "rep"), None),
        P(("lang", "rep"), None),
        P(("lang", "rep")),
        P(("lang", "rep")),
        P(None, "lang"),
        P(None, "lang"),
    )
    return jax.shard_map(
        per_device,
        mesh=mesh,
        in_specs=placed,
        out_specs=(
            P(("lang", "rep"), None),
            P(("lang", "rep"), None),
            P("rep", "lang"),
            P("rep", "lang"),
        ),
        check_vma=False,
    )
```

profile of v0, /device:TPU:46, one launch (start us, length us, event | category | flops | bytes accessed | tf_op | source)
XLA Modules:
  0.0 463.5 jit_solution(1449120945893397584)
XLA Ops:
  7.2 0.0 copy-start
  7.2 0.8 fusion.11
  7.9 1.6 scatter_custom_fusion
  9.6 0.1 reshape.40
  9.7 2.0 broadcast_in_dim.43
  11.7 16.4 %all-to-all-start = ((bf16[64,18,1024]{2,1,0:T(8,128)(2,1)}), bf16[64,18,1024]{2,1,0:T(8,128)(2,1)}, u32[]{:S(2)}, u32[]{:S(2)}) async-start(bf16[64,18,1024]{2,1,0:T(8,128)(2,1)} %bitcast.18), calls=%async_computation | async-start | bytes 6291456 | tf_op jit(solution)/shard_map/all_to_all | solution.py:52
  28.2 1.6 scatter_custom_fusion.1
  29.8 0.1 reshape.45
  29.9 97.4 %all-to-all-done = bf16[64,18,1024]{2,1,0:T(8,128)(2,1)} async-done(((bf16[64,18,1024]{2,1,0:T(8,128)(2,1)}), bf16[64,18,1024]{2,1,0:T(8,128)(2,1)}, u32[]{:S(2)}, u32[]{:S(2)}) %all-to-all-start) | async-done | bytes 2359328 | tf_op jit(solution)/shard_map/all_to_all | solution.py:52
  127.3 2.1 broadcast_in_dim.47
  129.4 9.1 %all-to-all-start.2 = ((bf16[64,18,1024]{2,1,0:T(8,128)(2,1)}), bf16[64,18,1024]{2,1,0:T(8,128)(2,1)}, u32[]{:S(2)}, u32[]{:S(2)}) async-start(bf16[64,18,1024]{2,1,0:T(8,128)(2,1)} %bitcast.19), calls=%async_computation.2 | async-start | bytes 6291456 | tf_op jit(solution)/shard_map/all_to_all | solution.py:68
  138.6 2.9 reshape.42
  141.5 0.0 copy-done
  141.5 0.0 copy-start.2
  141.5 3.3 multiply_convert_fusion
  144.9 0.0 copy-done.2
  144.9 84.0 %all-to-all-done.2 = bf16[64,18,1024]{2,1,0:T(8,128)(2,1)} async-done(((bf16[64,18,1024]{2,1,0:T(8,128)(2,1)}), bf16[64,18,1024]{2,1,0:T(8,128)(2,1)}, u32[]{:S(2)}, u32[]{:S(2)}) %all-to-all-start.2) | async-done | bytes 2359328 | tf_op jit(solution)/shard_map/all_to_all | solution.py:68
  228.9 2.9 reshape.47
  231.8 3.7 fusion
  235.5 0.0 copy-start.4
  235.5 1.1 copy-done.4
  236.6 2.8 convolution_convert_fusion
  239.4 4.3 reshape.48
  243.7 9.1 %all-to-all-start.3 = ((bf16[64,18,1024]{2,1,0:T(8,128)(2,1)}), bf16[64,18,1024]{2,1,0:T(8,128)(2,1)}, u32[]{:S(2)}, u32[]{:S(2)}) async-start(bf16[64,18,1024]{2,1,0:T(8,128)(2,1)} %reshape.48), calls=%async_computation.3 | async-start | bytes 6291456 | tf_op jit(solution)/shard_map/all_to_all | solution.py:97
  252.9 0.0 reduce-scatter.3.cloned.1.call-start
  252.9 5.0 %convolution_multiply_fusion.2 = f32[1024,512]{1,0:T(8,128)} fusion(bf16[1152,1024]{1,0:T(8,128)(2,1)} %copy-done.2, bf16[1152,512]{1,0:T(8,128)(2,1)} %copy-done.4), kind=kOutput, calls=%fused_computation.18 | convolution fusion | flops 1208483840 | bytes 5636096 | tf_op jit(solution)/shard_map/dot_general | solution.py:87
  257.9 0.0 reduce-scatter.3.cloned.1.call-update
  257.9 4.4 convolution_convert_fusion.1
  262.3 4.4 reshape.43
  266.7 66.6 %all-to-all-done.3 = bf16[64,18,1024]{2,1,0:T(8,128)(2,1)} async-done(((bf16[64,18,1024]{2,1,0:T(8,128)(2,1)}), bf16[64,18,1024]{2,1,0:T(8,128)(2,1)}, u32[]{:S(2)}, u32[]{:S(2)}) %all-to-all-start.3) | async-done | bytes 2359328 | tf_op jit(solution)/shard_map/all_to_all | solution.py:97
  333.2 14.2 %all-to-all-start.1 = ((bf16[64,18,1024]{2,1,0:T(8,128)(2,1)}), bf16[64,18,1024]{2,1,0:T(8,128)(2,1)}, u32[]{:S(2)}, u32[]{:S(2)}) async-start(bf16[64,18,1024]{2,1,0:T(8,128)(2,1)} %reshape.43), calls=%async_computation.1 | async-start | bytes 6291456 | tf_op jit(solution)/shard_map/all_to_all | solution.py:65
  347.4 0.0 copy-start.3
  347.4 0.0 reduce-scatter.5.cloned.1.call-start
  347.5 4.2 convolution_multiply_fusion.1
  351.6 0.0 reduce-scatter.5.cloned.1.call-update
  351.7 0.0 copy-done.3
  351.7 3.3 copy.13
  354.9 85.1 %all-to-all-done.1 = bf16[64,18,1024]{2,1,0:T(8,128)(2,1)} async-done(((bf16[64,18,1024]{2,1,0:T(8,128)(2,1)}), bf16[64,18,1024]{2,1,0:T(8,128)(2,1)}, u32[]{:S(2)}, u32[]{:S(2)}) %all-to-all-start.1) | async-done | bytes 2359328 | tf_op jit(solution)/shard_map/all_to_all | solution.py:65
  440.0 4.7 %copy.11 = bf16[8,8,18,1024]{3,1,2,0:T(8,128)(2,1)} copy(bf16[8,8,18,1024]{3,2,1,0:T(8,128)(2,1)} %bitcast.1) | data formatting | bytes 4718592 | tf_op jit(solution)/shard_map/reshape | solution.py:48
  444.7 2.2 gather_fusion.1
  446.8 0.0 copy-start.1
  446.8 4.0 gather_fusion
  450.8 0.0 copy-done.1
  450.8 4.9 %convert_reduce_fusion = (bf16[128,1024]{1,0:T(8,128)(2,1)S(1)}, bf16[128,1024]{1,0:T(8,128)(2,1)S(1)}) fusion(bf16[128,8,1024]{2,1,0:T(8,128)(2,1)S(1)} %copy-done.1, bf16[128,8,1024]{2,1,0:T(8,128)(2,1)} %gather_fusion), kind=kLoop, calls=%fused_computation.4 | loop fusion | flops 3932160 | bytes 4718592 | tf_op jit(solution)/shard_map/reduce_sum | solution.py:49
  455.7 0.9 select_convert_fusion
  456.7 0.0 reduce-scatter.3.cloned.1.call-done
  456.7 0.0 reduce-scatter.5.cloned.1.call-done
  (1 shorter events, 0.0 us)
Async XLA Ops:
  7.2 134.3 %copy-start = (bf16[1024,512]{1,0:T(8,128)(2,1)S(1)}, bf16[1024,512]{1,0:T(8,128)(2,1)}, u32[]{:S(2)}) copy-start(bf16[1024,512]{1,0:T(8,128)(2,1)} %param.10) | copy-start | bytes 3145732
  11.7 115.6 %all-to-all-start = ((bf16[64,18,1024]{2,1,0:T(8,128)(2,1)}), bf16[64,18,1024]{2,1,0:T(8,128)(2,1)}, u32[]{:S(2)}, u32[]{:S(2)}) async-start(bf16[64,18,1024]{2,1,0:T(8,128)(2,1)} %bitcast.18), calls=%async_computation | async-start | bytes 6291456 | tf_op jit(solution)/shard_map/all_to_all | solution.py:52
  129.4 99.5 %all-to-all-start.2 = ((bf16[64,18,1024]{2,1,0:T(8,128)(2,1)}), bf16[64,18,1024]{2,1,0:T(8,128)(2,1)}, u32[]{:S(2)}, u32[]{:S(2)}) async-start(bf16[64,18,1024]{2,1,0:T(8,128)(2,1)} %bitcast.19), calls=%async_computation.2 | async-start | bytes 6291456 | tf_op jit(solution)/shard_map/all_to_all | solution.py:68
  141.5 3.4 copy-start.2
  235.5 1.1 copy-start.4
  243.7 89.5 %all-to-all-start.3 = ((bf16[64,18,1024]{2,1,0:T(8,128)(2,1)}), bf16[64,18,1024]{2,1,0:T(8,128)(2,1)}, u32[]{:S(2)}, u32[]{:S(2)}) async-start(bf16[64,18,1024]{2,1,0:T(8,128)(2,1)} %reshape.48), calls=%async_computation.3 | async-start | bytes 6291456 | tf_op jit(solution)/shard_map/all_to_all | solution.py:97
  252.9 203.8 %reduce-scatter.3.cloned.1.call-start = ((), (), s32[]{:S(2)}) async-start(), calls=%async_computation.6 | async-start | bytes 2359296 | tf_op jit(solution)/shard_map/reduce_scatter | solution.py:86
  333.2 106.8 %all-to-all-start.1 = ((bf16[64,18,1024]{2,1,0:T(8,128)(2,1)}), bf16[64,18,1024]{2,1,0:T(8,128)(2,1)}, u32[]{:S(2)}, u32[]{:S(2)}) async-start(bf16[64,18,1024]{2,1,0:T(8,128)(2,1)} %reshape.43), calls=%async_computation.1 | async-start | bytes 6291456 | tf_op jit(solution)/shard_map/all_to_all | solution.py:65
  347.4 4.2 copy-start.3
  347.4 109.2 %reduce-scatter.5.cloned.1.call-start = ((), (), s32[]{:S(2)}) async-start(), calls=%async_computation.7 | async-start | bytes 2359296 | tf_op jit(solution)/shard_map/reduce_scatter | solution.py:74
  446.8 4.0 copy-start.1
Sparse Core Ops, SparseCore 0:
  258.0 37.0 reduce-scatter.2
  351.8 37.0 reduce-scatter.4
where the time goes:
time: 464 us
  waiting for transfers between devices  333 us (72%)
  starting transfers between devices  49 us (11%)
  local copies, waits for them, and re-layouts  37.3 us (8%)
  matrix products  23.4 us (5%)
  between operations  14.2 us (3%)
  other arithmetic  6.62 us (1%)
    all_to_all x1, waiting for transfers between devices, per_device(): lax.all_to_all(dispatch(tokens), 'lang', split_axis=0, concat_axis=0, til...  97.4 us
    all_to_all x1, waiting for transfers between devices, per_device(): lax.all_to_all(partial_rows, 'lang', split_axis=0, concat_axis=0, tiled=T...  85.1 us
    all_to_all x1, waiting for transfers between devices, per_device(): lax.all_to_all(dispatch(grad_out), 'lang', split_axis=0, concat_axis=0, t...  84 us
    all_to_all x1, waiting for transfers between devices, per_device(): lax.all_to_all(dx_part, 'lang', split_axis=0, concat_axis=0, tiled=True)  66.6 us
    all_to_all x1, starting transfers between devices, per_device(): lax.all_to_all(dispatch(tokens), 'lang', split_axis=0, concat_axis=0, til...  16.4 us
    all_to_all x1, starting transfers between devices, per_device(): lax.all_to_all(partial_rows, 'lang', split_axis=0, concat_axis=0, tiled=T...  14.2 us
  transfers between devices with their start and end apart: 6, of which 4 were waited for; matrix products, arithmetic and copies ran while one was open for 10% of the time, Pallas kernels for 0%

commit v1 on v0

v1 whole, which is shorter than its diff:
```python
import jax
import jax.numpy as jnp
from jax import lax
from jax.sharding import Mesh
from jax.sharding import PartitionSpec as P

MODULES = 8
TOK_DEV = 128
CAPACITY = 18


INV_ROOT_TWO = 0.7071067811865476
INV_ROOT_TAU = 0.3989422804014327


def gelu_value(values):
    return 0.5 * values * (1.0 + lax.erf(values * INV_ROOT_TWO))


def gelu_slope(values):
    return (
        0.5 * (1.0 + lax.erf(values * INV_ROOT_TWO))
        + values * jnp.exp(-0.5 * values * values) * INV_ROOT_TAU
    )


def per_device(tokens, grad_out, lang_ids, slot_ids, w_up, w_down_t):
    feature_width = tokens.shape[1]
    capacity = CAPACITY
    keep_mask = slot_ids < capacity
    target = jnp.where(keep_mask, lang_ids * capacity + slot_ids, MODULES * capacity)
    safe_slot = jnp.minimum(slot_ids, capacity - 1)
    token_scale = 1.0 / TOK_DEV

    def place(values):
        buffer = (
            jnp.zeros((MODULES * capacity, feature_width), values.dtype)
            .at[target]
            .set(values, mode="drop")
        )
        return buffer.reshape(MODULES, capacity, feature_width)

    def dispatch(values):
        by_y = lax.all_to_all(place(values), "ly", split_axis=0, concat_axis=0, tiled=True)
        every = lax.all_gather(by_y, "lz", axis=0, tiled=True)
        return every.reshape(-1, feature_width)

    def give_back(rows):
        parts = rows.astype(jnp.float32).reshape(-1, capacity, feature_width)
        summed = lax.psum_scatter(parts, "lz", scatter_dimension=0, tiled=True)
        summed = summed.astype(jnp.bfloat16)
        return lax.all_to_all(summed, "ly", split_axis=0, concat_axis=0, tiled=True)

    def collect(returned):
        picked = returned[lang_ids, safe_slot]
        return jnp.where(keep_mask[:, None], picked, jnp.zeros_like(picked))

    flat_tokens = dispatch(tokens)
    flat_grads = dispatch(grad_out)
    pre_flat = jnp.dot(flat_tokens, w_up, preferred_element_type=jnp.float32)
    hidden_flat = gelu_value(pre_flat).astype(jnp.bfloat16)
    partial_rows = lax.dot_general(
        hidden_flat, w_down_t, (((1,), (1,)), ((), ())), preferred_element_type=jnp.float32
    ).astype(jnp.bfloat16)
    returned = give_back(partial_rows)
    grad_down = lax.psum_scatter(
        lax.dot_general(
            flat_grads, hidden_flat, (((0,), (0,)), ((), ())), preferred_element_type=jnp.float32
        )
        * token_scale,
        "rep",
        scatter_dimension=0,
        tiled=True,
    )
    d_hidden = jnp.dot(flat_grads, w_down_t, preferred_element_type=jnp.float32)
    d_pre = (d_hidden * gelu_slope(pre_flat)).astype(jnp.bfloat16)
    grad_up = lax.psum_scatter(
        lax.dot_general(
            flat_tokens, d_pre, (((0,), (0,)), ((), ())), preferred_element_type=jnp.float32
        )
        * token_scale,
        "rep",
        scatter_dimension=0,
        tiled=True,
    )
    dx_part = lax.dot_general(
        d_pre, w_up, (((1,), (1,)), ((), ())), preferred_element_type=jnp.float32
    ).astype(jnp.bfloat16)
    dx_back = give_back(dx_part)
    return (collect(returned), collect(dx_back), grad_up, grad_down)


def solution(mesh):
    n_lang = mesh.shape["lang"]
    groups = n_lang // MODULES
    devices = mesh.devices.reshape(MODULES, groups, mesh.shape["rep"])
    split_mesh = Mesh(devices, ("ly", "lz", "rep"))
    rows = P(("ly", "lz", "rep"), None)
    ids = P(("ly", "lz", "rep"))
    cols = P(None, ("ly", "lz"))
    return jax.shard_map(
        per_device,
        mesh=split_mesh,
        in_specs=(rows, rows, ids, ids, cols, cols),
        out_specs=(rows, rows, P("rep", ("ly", "lz")), P("rep", ("ly", "lz"))),
        check_vma=False,
    )
```

time: 464 us -> 393 us (0.85)
  the two profiles are of different devices: /device:TPU:46 before, /device:TPU:6 now
where the time goes in v1:
time: 393 us; the launch traced here: 389 us
  waiting for transfers between devices  256 us (65%)
  local copies, waits for them, and re-layouts  37.6 us (10%)
  blocking collectives  37.6 us (10%)
  matrix products  24.5 us (6%)
  between operations  14.2 us (4%)
  starting transfers between devices  13.9 us (4%)
  other arithmetic  5.53 us (1%)
    reduce_scatter x2, waiting for transfers between devices, give_back(): summed = lax.psum_scatter(parts, 'lz', scatter_dimension=0, tiled=True)  127 us
    all_gather x2, waiting for transfers between devices, dispatch(): every = lax.all_gather(by_y, 'lz', axis=0, tiled=True)  63.8 us
    reduce_scatter x1, waiting for transfers between devices, per_device(): lax.psum_scatter(lax.dot_general(flat_grads, hidden_flat, (((0,), (0,)),...  40.9 us
    all_to_all x2, blocking collectives, dispatch(): lax.all_to_all(place(values), 'ly', split_axis=0, concat_axis=0, tiled=True)  37.6 us
    all_to_all x2, starting transfers between devices, give_back(): return lax.all_to_all(summed, 'ly', split_axis=0, concat_axis=0, tiled=True)  13.5 us
    all_to_all x2, waiting for transfers between devices, give_back(): return lax.all_to_all(summed, 'ly', split_axis=0, concat_axis=0, tiled=True)  13 us
    reshape x2, local copies, waits for them, and re-layouts, give_back(): parts = rows.astype(jnp.float32).reshape(-1, capacity, feature_width)  11.2 us
    reduce_scatter x1, waiting for transfers between devices, per_device(): lax.psum_scatter(lax.dot_general(flat_tokens, d_pre, (((0,), (0,)), ((),...  11.1 us
  transfers between devices with their start and end apart: 8, of which 7 were waited for; matrix products, arithmetic and copies ran while one was open for 10% of the time, Pallas kernels for 0%

profile of v1, /device:TPU:6, one launch (start us, length us, event | category | flops | bytes accessed | tf_op | source)
XLA Modules:
  0.0 389.2 jit_solution(12223299433012391685)
XLA Ops:
  7.2 0.0 copy-start
  7.2 0.0 all-gather.5.cloned.1.call-start
  7.2 0.8 fusion.13
  8.0 1.6 scatter_custom_fusion.1
  9.6 0.1 reshape.37
  9.7 21.6 %all_to_all.20 = bf16[8,18,1024]{2,1,0:T(8,128)(2,1)S(1)} all-to-all(bf16[8,18,1024]{2,1,0:T(8,128)(2,1)S(1)} %reshape.37), channel_id=1, replica_groups=mesh['ly'=8,'lz'=8,'rep'=8] {'ly'}, dimensions={0} | all-to-all | bytes 589824 | tf_op jit(solution)/shard_map/all_to_all | solution.py:44
  31.3 0.9 copy.17
  32.2 0.0 all-gather.5.cloned.1.call-update
  32.2 0.0 all-gather.3.cloned.1.call-start
  32.3 1.6 scatter_custom_fusion
  33.9 0.1 reshape.33
  34.0 16.0 %all_to_all.21 = bf16[8,18,1024]{2,1,0:T(8,128)(2,1)S(1)} all-to-all(bf16[8,18,1024]{2,1,0:T(8,128)(2,1)S(1)} %reshape.33), channel_id=1, replica_groups=mesh['ly'=8,'lz'=8,'rep'=8] {'ly'}, dimensions={0} | all-to-all | bytes 589824 | tf_op jit(solution)/shard_map/all_to_all | solution.py:44
  50.0 0.9 copy.14
  50.9 0.0 all-gather.3.cloned.1.call-update
  50.9 0.0 reduce-scatter.7.cloned.1.call-start
  50.9 25.9 %all-gather.5.cloned.1.call-done = bf16[64,18,1024]{2,0,1:T(8,128)(2,1)} async-done(((bf16[8,18,1024]{2,0,1:T(8,128)(2,1)}), bf16[64,18,1024]{2,0,1:T(8,128)(2,1)}) %all-gather.5.cloned.1.call-update) | async-done | bytes 2359312 | tf_op jit(solution)/shard_map/all_gather | solution.py:45
  76.8 4.7 %copy.18 = bf16[64,18,1024]{2,1,0:T(8,128)(2,1)} copy(bf16[64,18,1024]{2,0,1:T(8,128)(2,1)} %all-gather.5.cloned.1.call-done) | data formatting | bytes 4718592 | tf_op jit(solution)/shard_map/all_gather | solution.py:45
  81.5 2.9 reshape.38
  84.5 37.9 %all-gather.3.cloned.1.call-done = bf16[64,18,1024]{2,0,1:T(8,128)(2,1)} async-done(((bf16[8,18,1024]{2,0,1:T(8,128)(2,1)}), bf16[64,18,1024]{2,0,1:T(8,128)(2,1)}) %all-gather.3.cloned.1.call-update) | async-done | bytes 2359312 | tf_op jit(solution)/shard_map/all_gather | solution.py:45
  122.4 4.7 %copy.15 = bf16[64,18,1024]{2,1,0:T(8,128)(2,1)} copy(bf16[64,18,1024]{2,0,1:T(8,128)(2,1)} %all-gather.3.cloned.1.call-done) | data formatting | bytes 4718592 | tf_op jit(solution)/shard_map/all_gather | solution.py:45
  127.0 4.3 %reshape.34 = bf16[1152,1024]{1,0:T(8,128)(2,1)} reshape(bf16[64,18,1024]{2,1,0:T(8,128)(2,1)} %copy.15) | data formatting | bytes 4718592 | tf_op jit(solution)/shard_map/reshape | solution.py:46
  131.4 0.0 copy-done
  131.4 0.0 copy-start.2
  131.4 4.4 %multiply_convert_fusion = (bf16[1152,512]{1,0:T(8,128)(2,1)}, f32[1152,512]{1,0:T(8,128)S(1)}) fusion(bf16[1152,1024]{1,0:T(8,128)(2,1)} %reshape.34, bf16[1024,512]{1,0:T(8,128)(2,1)S(1)} %copy-done), kind=kOutput, calls=%fused_computation.15 | convolution fusion | flops 1210908672 | bytes 6946816 | tf_op jit(solution)/shard_map/dot_general | solution.py:60
  135.7 0.0 copy-done.2
  135.7 2.0 fusion.2
  137.8 0.0 copy-start.3
  137.8 1.0 copy-done.3
  138.8 3.7 fusion.1
  142.5 5.6 %reshape.44 = f32[64,18,1024]{2,1,0:T(8,128)} reshape(f32[1152,1024]{1,0:T(8,128)} %fusion.1) | data formatting | bytes 9437184 | tf_op jit(solution)/shard_map/reshape | solution.py:49
  148.0 0.0 reduce-scatter.7.cloned.1.call-update
  148.1 0.0 reduce-scatter.5.cloned.1.call-start
  148.1 5.1 %fusion = f32[1152,1024]{1,0:T(8,128)} fusion(bf16[1152,512]{1,0:T(8,128)(2,1)} %get-tuple-element.8, bf16[1024,512]{1,0:T(8,128)(2,1)} %param.11), kind=kOutput, calls=%fused_computation.6 | convolution fusion | flops 1210318848 | bytes 6946816 | tf_op jit(solution)/shard_map/dot_general | solution.py:62
  153.2 5.6 %reshape.42 = f32[64,18,1024]{2,1,0:T(8,128)} reshape(f32[1152,1024]{1,0:T(8,128)} %fusion) | data formatting | bytes 9437184 | tf_op jit(solution)/shard_map/reshape | solution.py:49
  158.8 0.0 reduce-scatter.5.cloned.1.call-update
  158.8 0.0 reduce-scatter.9.cloned.1.call-start
  158.9 5.2 %convolution_multiply_fusion.2 = f32[1024,512]{1,0:T(8,128)} fusion(bf16[1152,1024]{1,0:T(8,128)(2,1)} %reshape.34, bf16[1152,512]{1,0:T(8,128)(2,1)} %copy-done.3), kind=kOutput, calls=%fused_computation.18 | convolution fusion | flops 1208483840 | bytes 5636096 | tf_op jit(solution)/shard_map/dot_general | solution.py:78
  164.1 0.0 reduce-scatter.9.cloned.1.call-update
  164.1 0.2 reduce-scatter.11.cloned.1.call-start
  164.3 4.1 %convolution_multiply_fusion.1 = f32[1024,512]{1,0:T(8,128)} fusion(bf16[1152,1024]{1,0:T(8,128)(2,1)S(1)} %reshape.38, bf16[1152,512]{1,0:T(8,128)(2,1)} %get-tuple-element.8), kind=kOutput, calls=%fused_computation.17 | convolution fusion | flops 1208483840 | bytes 5636096 | tf_op jit(solution)/shard_map/dot_general | solution.py:67
  168.5 0.0 reduce-scatter.11.cloned.1.call-update
  168.5 0.0 copy-start.1
  168.5 56.3 %reduce-scatter.7.cloned.1.call-done = f32[8,18,1024]{2,1,0:T(8,128)} async-done(((f32[64,18,1024]{2,1,0:T(8,128)}), f32[8,18,1024]{2,1,0:T(8,128)}) %reduce-scatter.7.cloned.1.call-update) | async-done | bytes 589840 | tf_op jit(solution)/shard_map/reduce_scatter | solution.py:50
  224.8 1.9 convert_element_type.25
  226.8 6.7 %all-to-all-start.3 = ((bf16[8,18,1024]{2,1,0:T(8,128)(2,1)}), bf16[8,18,1024]{2,1,0:T(8,128)(2,1)S(1)}, u32[]{:S(2)}, u32[]{:S(2)}) async-start(bf16[8,18,1024]{2,1,0:T(8,128)(2,1)} %convert_element_type.25), calls=%async_computation.5 | async-start | bytes 786432 | tf_op jit(solution)/shard_map/all_to_all | solution.py:52
  233.5 70.7 %reduce-scatter.5.cloned.1.call-done = f32[8,18,1024]{2,1,0:T(8,128)} async-done(((f32[64,18,1024]{2,1,0:T(8,128)}), f32[8,18,1024]{2,1,0:T(8,128)}) %reduce-scatter.5.cloned.1.call-update) | async-done | bytes 589840 | tf_op jit(solution)/shard_map/reduce_scatter | solution.py:50
  304.2 1.9 convert_element_type.22
  306.1 0.0 all-to-all-done.3
  306.1 6.7 %all-to-all-start.1 = ((bf16[8,18,1024]{2,1,0:T(8,128)(2,1)}), bf16[8,18,1024]{2,1,0:T(8,128)(2,1)S(1)}, u32[]{:S(2)}, u32[]{:S(2)}) async-start(bf16[8,18,1024]{2,1,0:T(8,128)(2,1)} %convert_element_type.22), calls=%async_computation.2 | async-start | bytes 786432 | tf_op jit(solution)/shard_map/all_to_all | solution.py:52
  312.9 0.0 copy-done.1
  312.9 0.2 copy.19
  313.1 1.6 gather_fusion.1
  314.7 12.9 %all-to-all-done.1 = bf16[8,18,1024]{2,1,0:T(8,128)(2,1)S(1)} async-done(((bf16[8,18,1024]{2,1,0:T(8,128)(2,1)}), bf16[8,18,1024]{2,1,0:T(8,128)(2,1)S(1)}, u32[]{:S(2)}, u32[]{:S(2)}) %all-to-all-start.1) | async-done | bytes 294944 | tf_op jit(solution)/shard_map/all_to_all | solution.py:52
  327.6 0.2 copy.16
  327.8 1.6 gather_fusion
  329.4 0.9 broadcast_select_fusion
  330.3 11.1 %reduce-scatter.9.cloned.1.call-done = f32[128,512]{1,0:T(8,128)} async-done(((f32[1024,512]{1,0:T(8,128)}), f32[128,512]{1,0:T(8,128)}) %reduce-scatter.9.cloned.1.call-update) | async-done | bytes 262160 | tf_op jit(solution)/shard_map/reduce_scatter | solution.py:77
  341.4 40.9 %reduce-scatter.11.cloned.1.call-done = f32[128,512]{1,0:T(8,128)} async-done(((f32[1024,512]{1,0:T(8,128)}), f32[128,512]{1,0:T(8,128)}) %reduce-scatter.11.cloned.1.call-update) | async-done | bytes 262160 | tf_op jit(solution)/shard_map/reduce_scatter | solution.py:66
  (1 shorter events, 0.0 us)
Async XLA Ops:
  7.2 124.2 %copy-start = (bf16[1024,512]{1,0:T(8,128)(2,1)S(1)}, bf16[1024,512]{1,0:T(8,128)(2,1)}, u32[]{:S(2)}) copy-start(bf16[1024,512]{1,0:T(8,128)(2,1)} %param.10) | copy-start | bytes 3145732
  7.2 69.7 %all-gather.5.cloned.1.call-start = ((), (), s32[]{:S(2)}) async-start(), calls=%async_computation.10 | async-start | bytes 2654208 | tf_op jit(solution)/shard_map/all_gather | solution.py:45
  32.2 90.1 %all-gather.3.cloned.1.call-start = ((), (), s32[]{:S(2)}) async-start(), calls=%async_computation.8 | async-start | bytes 2654208 | tf_op jit(solution)/shard_map/all_gather | solution.py:45
  50.9 173.9 %reduce-scatter.7.cloned.1.call-start = ((), (), s32[]{:S(2)}) async-start(), calls=%async_computation.11 | async-start | bytes 7077888 | tf_op jit(solution)/shard_map/reduce_scatter | solution.py:50
  131.4 4.4 %copy-start.2 = (bf16[1024,512]{1,0:T(8,128)(2,1)S(1)}, bf16[1024,512]{1,0:T(8,128)(2,1)}, u32[]{:S(2)}) copy-start(bf16[1024,512]{1,0:T(8,128)(2,1)} %param.11) | copy-start | bytes 3145732
  137.8 1.0 copy-start.3
  148.1 156.1 %reduce-scatter.5.cloned.1.call-start = ((), (), s32[]{:S(2)}) async-start(), calls=%async_computation.9 | async-start | bytes 7077888 | tf_op jit(solution)/shard_map/reduce_scatter | solution.py:50
  158.8 182.6 %reduce-scatter.9.cloned.1.call-start = ((), (), s32[]{:S(2)}) async-start(), calls=%async_computation.12 | async-start | bytes 2359296 | tf_op jit(solution)/shard_map/reduce_scatter | solution.py:77
  164.1 218.2 %reduce-scatter.11.cloned.1.call-start = ((), (), s32[]{:S(2)}) async-start(), calls=%async_computation.13 | async-start | bytes 2359296 | tf_op jit(solution)/shard_map/reduce_scatter | solution.py:66
  168.5 144.4 %copy-start.1 = (s32[128]{0:T(128)S(1)}, s32[128]{0:T(128)}, u32[]{:S(2)}) copy-start(s32[128]{0:T(128)} %param.9) | copy-start | bytes 1540
  226.8 79.4 %all-to-all-start.3 = ((bf16[8,18,1024]{2,1,0:T(8,128)(2,1)}), bf16[8,18,1024]{2,1,0:T(8,128)(2,1)S(1)}, u32[]{:S(2)}, u32[]{:S(2)}) async-start(bf16[8,18,1024]{2,1,0:T(8,128)(2,1)} %convert_element_type.25), calls=%async_computation.5 | async-start | bytes 786432 | tf_op jit(solution)/shard_map/all_to_all | solution.py:52
  306.1 21.5 %all-to-all-start.1 = ((bf16[8,18,1024]{2,1,0:T(8,128)(2,1)}), bf16[8,18,1024]{2,1,0:T(8,128)(2,1)S(1)}, u32[]{:S(2)}, u32[]{:S(2)}) async-start(bf16[8,18,1024]{2,1,0:T(8,128)(2,1)} %convert_element_type.22), calls=%async_computation.2 | async-start | bytes 786432 | tf_op jit(solution)/shard_map/all_to_all | solution.py:52
Sparse Core Ops, SparseCore 0:
  32.3 44.4 all-gather.4
  78.9 43.4 all-gather.2
  148.2 76.5 reduce-scatter.6
  227.5 76.6 reduce-scatter.4
  307.5 33.9 reduce-scatter.8
  344.7 37.5 reduce-scatter.10
